TPU v7x, 32 devices: a whole 2x2x4 slice. The times are simulated.
32 devices in a mesh: seq: 8 (over z, y), blk: 4 (over x, core).
Axes of the slice: x: 2, y: 2, z: 4, core: 2. Of those that a mesh axis runs over, the one named last changes fastest.
Arguments:
- q_latent: bfloat16 [64, 128, 512], P('blk', 'seq'), may hold values from -16 to 16
- q_rope: bfloat16 [64, 64, 128], P('blk', None, 'seq'), may hold values from -9 to 9
- cache_latent: bfloat16 [16384, 512], P(('seq', 'blk')), may hold values from -8 to 8
- cache_rope: bfloat16 [64, 16384], P(None, ('seq', 'blk')), may hold values from -6 to 6
- draft_latent: bfloat16 [64, 512], replicated, may hold values from -8 to 8
- draft_rope: bfloat16 [64, 64], replicated, may hold values from -6 to 6
- ancestors: int32 [64, 64], replicated, may hold values from 0 to 1, as said below
- valid_length: int32 [], replicated, may hold values from 8192 to 16384
- accepted: int32 [64], P('blk'), may hold values from 0 to 1, as said below
- w_value: bfloat16 [128, 512, 128], P('seq'), may hold values from -3 to 3
Outputs:
- attended: bfloat16 [64, 128, 128], P('blk', 'seq')
- accepted_total: int32 [], replicated
Inputs may be any that keep to these rules, and one draw needn't show every extreme that they name: Node 0 is the root; every other node's parent has a lower index; ancestors[i, j] = 1 exactly when j is i or an ancestor of i. accepted is the row of ancestors of one node of the tree: that node and all of its ancestors.
All inputs are finite; a program needn't handle non-finite values.
Results may differ from a plain program's by a relative error of at most 0.02.
Values may be sent and summed in bfloat16 or wider, within the bound.
A program may use at most 64 MiB of HBM per device.

v0:
```python
import jax
import jax.numpy as jnp
from jax import lax
from jax.sharding import PartitionSpec as P

ROPE = 64
VDIM = 128


def cache_block(query, qrot, cache_latent, cache_rope, live, scale):
    scores = jnp.einsum("thl,sl->hts", query, cache_latent, preferred_element_type=jnp.float32)
    scores = scores + jnp.einsum(
        "trh,rs->hts", qrot, cache_rope, preferred_element_type=jnp.float32
    )
    scores = jnp.where(live[None, None, :], scores * scale, -1e30)
    peak = jnp.max(scores, axis=2)
    weights = jnp.exp(scores - peak[:, :, None])
    total = jnp.sum(weights, axis=2)
    latent = jnp.einsum(
        "hts,sl->htl",
        weights.astype(jnp.bfloat16),
        cache_latent,
        preferred_element_type=jnp.float32,
    )
    return (latent, peak, total)


def combine_pieces(pieces, peaks, totals):
    merged_peak = jnp.max(peaks, axis=0)
    factor = jnp.exp(peaks - merged_peak[None])
    merged = jnp.sum(pieces * factor[:, :, :, None], axis=0)
    merged_total = jnp.sum(totals * factor, axis=0)
    return (merged, merged_total, merged_peak)


def shards(
    q_latent,
    q_rope,
    cache_latent,
    cache_rope,
    draft_latent,
    draft_rope,
    ancestors,
    valid_length,
    accepted,
    w_value,
):
    scale = (VDIM + ROPE) ** (-0.5)
    own_tokens = q_latent.shape[0]
    rows = cache_latent.shape[0]
    token_first = lax.axis_index("blk") * own_tokens
    queries, rotary = (
        lax.all_gather(q_latent, "blk", axis=0, tiled=True),
        lax.all_gather(q_rope, "blk", axis=0, tiled=True),
    )
    queries, rotary = (
        lax.all_gather(queries, "seq", axis=1, tiled=True),
        lax.all_gather(rotary, "seq", axis=2, tiled=True),
    )
    keys, key_rope = (cache_latent, cache_rope)
    start = lax.axis_index(("seq", "blk")) * rows
    heads = queries.shape[1]
    draft = queries.shape[0]
    width = min(16, heads)
    live = start + jnp.arange(keys.shape[0], dtype=jnp.int32) < valid_length

    def one_block(index):
        first = index * width
        query = lax.dynamic_slice_in_dim(queries, first, width, 1)
        qrot = lax.dynamic_slice_in_dim(rotary, first, width, 2)
        return cache_block(query, qrot, keys, key_rope, live, scale)

    latent, peak, total = lax.map(one_block, jnp.arange(heads // width, dtype=jnp.int32))
    latent = latent.reshape(heads, draft, latent.shape[-1])
    peak = peak.reshape(heads, draft)
    total = total.reshape(heads, draft)
    pieces, peaks, totals = (
        lax.all_to_all(
            lax.all_to_all(latent[None], "seq", split_axis=1, concat_axis=0, tiled=True),
            "blk",
            split_axis=2,
            concat_axis=0,
            tiled=True,
        ),
        lax.all_to_all(
            lax.all_to_all(peak[None], "seq", split_axis=1, concat_axis=0, tiled=True),
            "blk",
            split_axis=2,
            concat_axis=0,
            tiled=True,
        ),
        lax.all_to_all(
            lax.all_to_all(total[None], "seq", split_axis=1, concat_axis=0, tiled=True),
            "blk",
            split_axis=2,
            concat_axis=0,
            tiled=True,
        ),
    )
    merged, merged_total, merged_peak = combine_pieces(pieces, peaks, totals)
    draft_score = jnp.einsum(
        "thl,jl->htj", q_latent, draft_latent, preferred_element_type=jnp.float32
    )
    draft_score = draft_score + jnp.einsum(
        "trh,rj->htj", q_rope, draft_rope, preferred_element_type=jnp.float32
    )
    tree = lax.dynamic_slice_in_dim(ancestors, token_first, own_tokens, 0)
    draft_score = jnp.where(tree[None, :, :] == 1, draft_score * scale, -1e30)
    best = jnp.maximum(merged_peak, jnp.max(draft_score, axis=2))
    keep = jnp.exp(merged_peak - best)
    draft_weights = jnp.exp(draft_score - best[:, :, None])
    whole_total = merged_total * keep + jnp.sum(draft_weights, axis=2)
    combined = merged * keep[:, :, None]
    combined = combined + jnp.einsum(
        "htj,jl->htl",
        draft_weights.astype(jnp.bfloat16),
        draft_latent,
        preferred_element_type=jnp.float32,
    )
    combined = combined / whole_total[:, :, None]
    attended = jnp.einsum(
        "htl,hlv->thv", combined, w_value.astype(jnp.float32), precision=lax.Precision.HIGHEST
    )
    accepted_total = lax.psum(jnp.sum(accepted), "blk")
    return (attended.astype(jnp.bfloat16), accepted_total)


def solution(mesh):
    return jax.shard_map(
        shards,
        mesh=mesh,
        in_specs=(
            P("blk", "seq", None),
            P("blk", None, "seq"),
            P(("seq", "blk"), None),
            P(None, ("seq", "blk")),
            P(),
            P(),
            P(),
            P(),
            P("blk"),
            P("seq", None, None),
        ),
        out_specs=(P("blk", "seq", None), P()),
        check_vma=False,
    )
```

profile of v0, /device:TPU:25, one launch (start us, length us, event | category | flops | bytes accessed | tf_op | source)
XLA Modules:
  0.0 896.7 jit_solution(2978225908263926256)
XLA Ops:
  8.0 7.9 all_gather.14
  15.9 11.7 %all-gather.4.cloned.1.call-done = bf16[64,16,512]{2,1,0:T(8,128)(2,1)} async-done(((bf16[16,16,512]{2,1,0:T(8,128)(2,1)}), bf16[64,16,512]{2,1,0:T(8,128)(2,1)}) %all-gather.4.cloned.1.call-update) | async-done | bytes 1048592 | tf_op jit(solution)/shard_map/all_gather | solution.py:53
  27.7 50.1 %all-gather.8.cloned.1.call-done = bf16[64,64,128]{1,2,0:T(8,128)(2,1)} async-done(((bf16[64,64,16]{1,2,0:T(8,128)(2,1)}), bf16[64,64,128]{1,2,0:T(8,128)(2,1)}) %all-gather.8.cloned.1.call-update) | async-done | bytes 1048592 | tf_op jit(solution)/shard_map/all_gather | solution.py:58
  77.8 124.9 %all-gather.6.cloned.1.call-done = bf16[64,128,512]{2,1,0:T(8,128)(2,1)} async-done(((bf16[64,16,512]{2,1,0:T(8,128)(2,1)}), bf16[64,128,512]{2,1,0:T(8,128)(2,1)}) %all-gather.6.cloned.1.call-update) | async-done | bytes 8388624 | tf_op jit(solution)/shard_map/all_gather | solution.py:57
  202.7 65.1 %while.15 = (s32[]{:T(128)}, f32[8,16,64,512]{3,2,1,0:T(8,128)}, f32[8,16,64]{2,1,0:T(8,128)S(1)}, f32[8,16,64]{2,1,0:T(8,128)S(1)}, s32[8]{0:T(128)S(1)}, /*ind...) while((s32[]{:T(128)}, f32[8,16,64,512]{3,2,1,0:T(8,128)}, ...), condition=%wide.region_3.4_spmd.clone, body=%wide.region_0.3_spmd.clone.sunk | while | flops 1144519680 | bytes 17168120 | solution.py:73
  205.9 2.1 bitcast_reduce_fusion.3
  208.5 2.2 bitcast_dynamic-update-slice_fusion.2
  214.0 2.1 bitcast_reduce_fusion.3
  216.7 2.1 bitcast_dynamic-update-slice_fusion.2
  222.1 2.1 bitcast_reduce_fusion.3
  224.8 2.2 bitcast_dynamic-update-slice_fusion.2
  230.3 2.1 bitcast_reduce_fusion.3
  232.9 2.2 bitcast_dynamic-update-slice_fusion.2
  238.4 2.1 bitcast_reduce_fusion.3
  241.1 2.2 bitcast_dynamic-update-slice_fusion.2
  246.6 2.1 bitcast_reduce_fusion.3
  249.3 2.1 bitcast_dynamic-update-slice_fusion.2
  254.7 2.1 bitcast_reduce_fusion.3
  257.4 2.2 bitcast_dynamic-update-slice_fusion.2
  262.9 2.1 bitcast_reduce_fusion.3
  265.5 2.2 bitcast_dynamic-update-slice_fusion.2
  270.0 4.6 all-to-all-start.2
  277.3 6.1 all-to-all-start.4
  284.5 1.4 all-to-all-done.4
  285.9 9.4 %all_to_all.81 = f32[4,1,2048]{2,1,0:T(1,128)S(1)} all-to-all(f32[4,1,2048]{2,1,0:T(1,128)S(1)} %reshape.55), channel_id=1, replica_groups=mesh['seq'=8,'blk'=4] {'blk'}, dimensions={0} | all-to-all | bytes 65536 | tf_op jit(solution)/shard_map/all_to_all | solution.py:85
  295.3 8.7 all-to-all-start
  305.7 360.3 %all-to-all-done = f32[1,128,64,512]{3,2,0,1:T(8,128)} async-done(((f32[1,128,64,512]{3,2,0,1:T(8,128)}), f32[1,128,64,512]{3,2,0,1:T(8,128)}, u32[]{:S(2)}, u32[]{:S(2)}) %all-to-all-start) | async-done | bytes 16777248 | tf_op jit(solution)/shard_map/all_to_all | solution.py:79
  666.1 3.7 all-to-all-start.5
  669.8 17.7 %copy.39 = f32[8,16,64,512]{3,1,0,2:T(8,128)} copy(f32[8,16,64,512]{3,2,1,0:T(8,128)} %bitcast.1) | data formatting | bytes 33554432 | tf_op jit(solution)/shard_map/all_to_all | solution.py:79
  687.6 7.1 all-to-all-start.1
  695.4 182.0 %psum.7 = s32[]{:T(128)} all-reduce(s32[]{:T(128)} %reduce_sum.48), channel_id=1, replica_groups=mesh['seq'=8,'blk'=4] {'blk'}, use_global_device_ids=true, to_apply=%region_10.11 | all-reduce | flops 1 | bytes 8 | tf_op jit(solution)/shard_map/psum | solution.py:124
  881.5 6.7 multiply_reduce_fusion
  (132 shorter events, 41.5 us)
Async XLA Ops:
  7.2 881.4 %copy-start = (bf16[16,512,128]{2,1,0:T(8,128)(2,1)S(1)}, bf16[16,512,128]{2,1,0:T(8,128)(2,1)}, u32[]{:S(2)}) copy-start(bf16[16,512,128]{2,1,0:T(8,128)(2,1)} %param.21) | copy-start | bytes 6291460
  7.2 20.5 %all-gather.4.cloned.1.call-start = ((), (), s32[]{:S(2)}) async-start(), calls=%async_computation.6 | async-start | bytes 1310720 | tf_op jit(solution)/shard_map/all_gather | solution.py:53
  7.9 69.9 %all-gather.8.cloned.1.call-start = ((), (), s32[]{:S(2)}) async-start(), calls=%async_computation.8 | async-start | bytes 2359296 | tf_op jit(solution)/shard_map/all_gather | solution.py:58
  15.9 186.9 %all-gather.6.cloned.1.call-start = ((), (), s32[]{:S(2)}) async-start(), calls=%async_computation.7 | async-start | bytes 9437184 | tf_op jit(solution)/shard_map/all_gather | solution.py:57
  202.7 3.2 copy-start.1
  210.9 3.2 copy-start.1
  219.0 3.2 copy-start.1
  227.1 3.2 copy-start.1
  235.2 3.2 copy-start.1
  243.4 3.2 copy-start.1
  251.5 3.2 copy-start.1
  259.7 3.2 copy-start.1
  270.0 7.3 all-to-all-start.2
  277.3 8.6 all-to-all-start.4
  295.3 370.8 %all-to-all-start = ((f32[1,128,64,512]{3,2,0,1:T(8,128)}), f32[1,128,64,512]{3,2,0,1:T(8,128)}, u32[]{:S(2)}, u32[]{:S(2)}) async-start(f32[1,128,64,512]{3,2,0,1:T(8,128)} %bitcast.95), calls=%async_computation | async-start | bytes 33554432 | tf_op jit(solution)/shard_map/all_to_all | solution.py:79
  666.1 21.5 %all-to-all-start.5 = ((f32[4,1,2048]{2,1,0:T(1,128)}), f32[4,1,2048]{2,1,0:T(1,128)S(1)}, u32[]{:S(2)}, u32[]{:S(2)}) async-start(f32[4,1,2048]{2,1,0:T(1,128)} %reshape.59), calls=%async_computation.5 | async-start | bytes 65536 | tf_op jit(solution)/shard_map/all_to_all | solution.py:92
  687.6 7.2 copy-start.6
  687.6 190.5 %copy-start.3 = (bf16[16,64,16]{1,2,0:T(8,128)(2,1)S(1)}, bf16[16,64,16]{1,2,0:T(8,128)(2,1)}, u32[]{:S(2)}) copy-start(bf16[16,64,16]{1,2,0:T(8,128)(2,1)} %param.13) | copy-start | bytes 98308
  687.6 190.5 %copy-start.5 = (bf16[64,64]{1,0:T(8,128)(2,1)S(1)}, bf16[64,64]{1,0:T(8,128)(2,1)}, u32[]{:S(2)}) copy-start(bf16[64,64]{1,0:T(8,128)(2,1)} %param.17) | copy-start | bytes 24580
  687.6 190.7 %copy-start.2 = (bf16[16,16,512]{2,1,0:T(8,128)(2,1)S(1)}, bf16[16,16,512]{2,1,0:T(8,128)(2,1)}, u32[]{:S(2)}) copy-start(bf16[16,16,512]{2,1,0:T(8,128)(2,1)} %param.12) | copy-start | bytes 786436
  687.6 190.7 %copy-start.4 = (bf16[64,512]{1,0:T(8,128)(2,1)S(1)}, bf16[64,512]{1,0:T(8,128)(2,1)}, u32[]{:S(2)}) copy-start(bf16[64,512]{1,0:T(8,128)(2,1)} %param.16) | copy-start | bytes 196612
  687.6 193.9 %all-to-all-start.1 = ((f32[8,16,64,512]{3,1,0,2:T(8,128)}), f32[8,16,64,512]{3,1,0,2:T(8,128)}, u32[]{:S(2)}, u32[]{:S(2)}) async-start(f32[8,16,64,512]{3,1,0,2:T(8,128)} %copy.39), calls=%async_computation.1 | async-start | bytes 33554432 | tf_op jit(solution)/shard_map/all_to_all | solution.py:78
Sparse Core Ops, SparseCore 0:
  9.5 18.0 all-gather.3
  29.7 48.1 all-gather.7
  80.0 122.6 all-gather.5
where the time goes:
time: 901 us; the launch traced here: 897 us
  waiting for transfers between devices  550 us (61%)
  blocking collectives  199 us (22%)
  matrix products  46.9 us (5%)
  starting transfers between devices  30.3 us (3%)
  local copies, waits for them, and re-layouts  28.4 us (3%)
  other arithmetic  22.8 us (3%)
  between operations  14 us (2%)
    all_to_all x1, waiting for transfers between devices, shards(): lax.all_to_all(latent[None], 'seq', split_axis=1, concat_axis=0, tiled=True)  360 us
    psum x1, blocking collectives, shards(): accepted_total = lax.psum(jnp.sum(accepted), 'blk')  182 us
    all_gather x1, waiting for transfers between devices, shards(): lax.all_gather(queries, 'seq', axis=1, tiled=True)  125 us
    all_gather x1, waiting for transfers between devices, shards(): lax.all_gather(rotary, 'seq', axis=2, tiled=True)  50.1 us
  transfers between devices with their start and end apart: 8, of which 6 were waited for; matrix products, arithmetic and copies ran while one was open for 3% of the time, Pallas kernels for 0%

commit v1 on v0

v1 whole, which is shorter than its diff:
```python
import functools

import jax
import jax.numpy as jnp
from jax import lax
from jax.experimental import pallas as pl
from jax.experimental.pallas import tpu as pltpu
from jax.sharding import PartitionSpec as P

ROPE = 64
VDIM = 128
NEG = -1e30
F32 = jnp.float32
BF16 = jnp.bfloat16
NT = (((1,), (1,)), ((), ()))


def inner_extent(n_seq):
    side = 1
    while 2 * side * side * 4 <= n_seq:
        side *= 2
    return side if n_seq % side == 0 else 1


def kernel(
    nz,
    ny,
    nb,
    tokens,
    heads,
    valid_ref,
    accepted_ref,
    q_ref,
    qr_ref,
    kl_ref,
    kr_ref,
    dl_ref,
    dr_ref,
    anc_ref,
    w_ref,
    out_ref,
    count_ref,
    kbuf,
    qbuf,
    qrbuf,
    wbuf,
    top,
    tot,
    acc,
    xbuf,
    outf,
    osend,
    ssend,
    orecv,
    srecv,
    local_sem,
    qsend_sem,
    qrecv_sem,
    up_sem,
    down_sem,
    side_sem,
    recv_sem,
    xsend_sem,
    xrecv_sem,
):
    scale = (VDIM + ROPE) ** (-0.5)
    rows = tokens * heads
    keys, latent = kl_ref.shape
    seq = lax.axis_index("seq")
    blk = lax.axis_index("blk")
    z, y = seq // ny, seq % ny

    fills = [
        pltpu.make_async_copy(kl_ref, kbuf.at[seq, pl.ds(0, keys)], local_sem.at[0]),
        pltpu.make_async_copy(kr_ref, kbuf.at[seq, pl.ds(keys, ROPE)], local_sem.at[1]),
        pltpu.make_async_copy(q_ref, qbuf.at[blk], local_sem.at[2]),
        pltpu.make_async_copy(qr_ref, qrbuf.at[blk], local_sem.at[3]),
        pltpu.make_async_copy(w_ref, wbuf, local_sem.at[4]),
    ]
    for fill in fills:
        fill.start()

    def blk_peer(k):
        return {"blk": lax.rem(blk + k, nb)}

    def side_peer(j):
        return {"seq": z * ny + lax.rem(y + j, ny)}

    barrier = pltpu.get_barrier_semaphore()
    for k in range(1, nb):
        pl.semaphore_signal(barrier, inc=1, device_id=blk_peer(k))
    for j in range(1, ny):
        pl.semaphore_signal(barrier, inc=1, device_id=side_peer(j))

    @pl.when(z < nz - 1)
    def _():
        pl.semaphore_signal(barrier, inc=1, device_id={"seq": seq + ny})

    @pl.when(z > 0)
    def _():
        pl.semaphore_signal(barrier, inc=1, device_id={"seq": seq - ny})

    arrivals = (nb - 1) + (ny - 1) + jnp.where(z < nz - 1, 1, 0) + jnp.where(z > 0, 1, 0)
    pl.semaphore_wait(barrier, arrivals)

    above, below = nz - 1 - z, z
    near = jnp.minimum(above, below)

    def plane(k):
        odd = lax.rem(k, 2)
        close = jnp.where(odd == 1, z + (k + 1) // 2, z - k // 2)
        far = jnp.where(above > below, z + (k - near), z - (k - near))
        return jnp.where(k <= 2 * near, close, far)

    def remote(src, dst, send, recv, where):
        return pltpu.make_async_remote_copy(
            src_ref=src, dst_ref=dst, send_sem=send, recv_sem=recv,
            device_id=where, device_id_type=pl.DeviceIdType.MESH,
        )

    def piece(p, send, where):
        return remote(kbuf.at[p], kbuf.at[p], send, recv_sem.at[p], where)

    def up(k):
        return piece(plane(k) * ny + y, up_sem.at[k], {"seq": jnp.minimum(seq + ny, nz * ny - 1)})

    def down(k):
        return piece(plane(k) * ny + y, down_sem.at[k], {"seq": jnp.maximum(seq - ny, 0)})

    def side(k, j):
        return piece(plane(k) * ny + y, side_sem.at[k * max(ny - 1, 1) + j - 1], side_peer(j))

    def sends(k, act):
        @pl.when(jnp.logical_and(plane(k) <= z, z < nz - 1))
        def _():
            act(up(k))

        @pl.when(jnp.logical_and(plane(k) >= z, z > 0))
        def _():
            act(down(k))

        for j in range(1, ny):
            act(side(k, j))

    fills[0].wait()
    fills[1].wait()
    sends(0, lambda c: c.start())

    def query_copies(k):
        return (
            remote(q_ref, qbuf.at[blk], qsend_sem.at[2 * k - 2], qrecv_sem.at[2 * k - 2], blk_peer(k)),
            remote(qr_ref, qrbuf.at[blk], qsend_sem.at[2 * k - 1], qrecv_sem.at[2 * k - 1], blk_peer(k)),
        )

    for k in range(1, nb):
        for c in query_copies(k):
            c.start()

    top[...] = jnp.full_like(top, NEG)
    tot[...] = jnp.zeros_like(tot)

    def clear(i, carry):
        acc[pl.ds(i * rows, rows), :] = jnp.zeros((rows, latent), F32)
        return carry

    lax.fori_loop(0, nb, clear, 0)
    fills[2].wait()
    fills[3].wait()
    nodes = dl_ref.shape[0]
    dscore = lax.dot_general(qbuf[blk], dl_ref[...], NT, preferred_element_type=F32)
    dscore = dscore + jnp.dot(qrbuf[blk], dr_ref[...], preferred_element_type=F32)
    row = lax.broadcasted_iota(jnp.int32, (rows, tokens), 0)
    first = lax.broadcasted_iota(jnp.int32, (rows, tokens), 1) * heads
    spread = jnp.where(jnp.logical_and(row >= first, row < first + heads), 1.0, 0.0)
    tree = anc_ref[pl.ds(pl.multiple_of(blk * tokens, tokens), tokens), :].astype(F32)
    tree = jnp.dot(spread, tree, preferred_element_type=F32)
    dscore = jnp.where(tree > 0.5, dscore * scale, NEG)
    dpeak = jnp.max(dscore, axis=1, keepdims=True)
    dweight = jnp.exp(dscore - dpeak)
    top[blk] = dpeak
    tot[blk] = jnp.sum(dweight, axis=1, keepdims=True)
    acc[pl.ds(pl.multiple_of(blk * rows, rows), rows), :] = jnp.dot(
        dweight.astype(BF16), dl_ref[...], preferred_element_type=F32
    )
    valid = valid_ref[0]

    def attend(p):
        start = (p * nb + blk) * keys
        live = start + lax.broadcasted_iota(jnp.int32, (1, keys), 1) < valid

        def block(i, carry):
            key = kbuf[p, pl.ds(0, keys), :]
            score = lax.dot_general(qbuf[i], key, NT, preferred_element_type=F32)
            score = score + jnp.dot(
                qrbuf[i], kbuf[p, pl.ds(keys, ROPE), :], preferred_element_type=F32
            )
            score = jnp.where(live, score * scale, NEG)
            old = top[i]
            new = jnp.maximum(old, jnp.max(score, axis=1, keepdims=True))
            weight = jnp.exp(score - new)
            fade = jnp.exp(old - new)
            top[i] = new
            tot[i] = tot[i] * fade + jnp.sum(weight, axis=1, keepdims=True)
            at = pl.ds(pl.multiple_of(i * rows, rows), rows)
            acc[at, :] = acc[at, :] * fade + jnp.dot(
                weight.astype(BF16), key, preferred_element_type=F32
            )
            return carry

        lax.fori_loop(0, nb, block, 0)

    def step(k, carry):
        @pl.when(jnp.logical_and(k >= 1, k < nz))
        def _():
            p = plane(k) * ny + y
            piece(p, recv_sem.at[p], {"seq": seq}).wait_recv()
            sends(k, lambda c: c.start())

        @pl.when(k == 1)
        def _():
            for j in range(1, nb):
                for c in query_copies(j):
                    c.wait_recv()

        @pl.when(k <= nz)
        def _():
            attend(plane(k - 1) * ny + y)

        @pl.when(k >= 2)
        def _():
            def one(j, inner):
                p = plane(k - 2) * ny + lax.rem(y + j, ny)
                piece(p, recv_sem.at[p], {"seq": seq}).wait_recv()
                attend(p)
                return inner

            lax.fori_loop(1, ny, one, 0)

        return carry

    lax.fori_loop(1, nz + 2, step, 0)

    def finish(i, carry):
        at = pl.ds(pl.multiple_of(i * rows, rows), rows)
        scaled = acc[at, :] / tot[i]
        for c in range(latent // 128):
            xbuf[c, at, :] = scaled[:, c * 128 : (c + 1) * 128]
        lse = top[i] + jnp.log(tot[i])
        flat = jnp.transpose(jnp.broadcast_to(lse, (rows, 128)))
        ssend[i, pl.ds(0, 8), :] = flat[0:8]
        return carry

    lax.fori_loop(0, nb, finish, 0)
    fills[4].wait()
    for h in range(heads):
        x = jnp.concatenate(
            [
                xbuf.at[c][pl.ds(h, nb * tokens, stride=heads), :]
                for c in range(latent // 128)
            ],
            axis=1,
        ).astype(BF16)
        outf[pl.ds(h, nb * tokens, stride=heads), :] = jnp.dot(
            x, wbuf[h], preferred_element_type=F32
        )
    mine = accepted_ref[0]
    for t in range(1, tokens):
        mine = mine + accepted_ref[t]
    count = jnp.full((8, rows), mine, jnp.int32).astype(F32)
    for i in range(nb):
        osend[i] = outf[pl.ds(i * rows, rows), :].astype(BF16)
        ssend[i, pl.ds(8, 8), :] = count

    def result_copies(k):
        to = lax.rem(blk + k, nb)
        return (
            remote(osend.at[to], orecv.at[k - 1], xsend_sem.at[2 * k - 2], xrecv_sem.at[2 * k - 2], blk_peer(k)),
            remote(ssend.at[to], srecv.at[k - 1], xsend_sem.at[2 * k - 1], xrecv_sem.at[2 * k - 1], blk_peer(k)),
        )

    for k in range(1, nb):
        for c in result_copies(k):
            c.start()

    def column(flat):
        return jnp.transpose(jnp.broadcast_to(flat, (128, rows)))

    for k in range(1, nb):
        for c in result_copies(k):
            c.wait_recv()
    lses = [column(ssend[blk, pl.ds(0, 1), :])]
    lses += [column(srecv[k - 1, pl.ds(0, 1), :]) for k in range(1, nb)]
    peak = functools.reduce(jnp.maximum, lses)
    weights = [jnp.exp(v - peak) for v in lses]
    whole = functools.reduce(jnp.add, weights)
    merged = weights[0] * outf[pl.ds(pl.multiple_of(blk * rows, rows), rows), :]
    for k in range(1, nb):
        merged = merged + weights[k] * orecv[k - 1].astype(F32)
    out_ref[...] = (merged / whole).astype(out_ref.dtype)
    for k in range(1, nb):
        count = count + srecv[k - 1, pl.ds(8, 8), :]
    count_ref[...] = count[:, 0:1].astype(jnp.int32)

    def drain(k, carry):
        sends(k, lambda c: c.wait_send())
        return carry

    lax.fori_loop(0, nz, drain, 0)
    for k in range(1, nb):
        for c in query_copies(k):
            c.wait_send()
        for c in result_copies(k):
            c.wait_send()


def shards(n_seq, n_blk, q_latent, q_rope, cache_latent, cache_rope, draft_latent, draft_rope,
           ancestors, valid_length, accepted, w_value):
    tokens, heads, latent = q_latent.shape
    rows = tokens * heads
    keys = cache_latent.shape[0]
    ny = inner_extent(n_seq)
    nz = n_seq // ny
    side = max(ny - 1, 1)
    assert keys == latent
    query = q_latent.reshape(rows, latent)
    rotary = jnp.transpose(q_rope, (0, 2, 1)).reshape(rows, ROPE)
    vmem = pl.BlockSpec(memory_space=pltpu.VMEM)
    smem = pl.BlockSpec(memory_space=pltpu.SMEM)
    hbm = pl.BlockSpec(memory_space=pl.ANY)
    dma = pltpu.SemaphoreType.DMA
    out, count = pl.pallas_call(
        functools.partial(kernel, nz, ny, n_blk, tokens, heads),
        out_shape=(
            jax.ShapeDtypeStruct((rows, VDIM), BF16),
            jax.ShapeDtypeStruct((8, 1), jnp.int32),
        ),
        in_specs=[smem, smem, hbm, hbm, hbm, hbm, vmem, vmem, vmem, hbm],
        out_specs=(vmem, vmem),
        scratch_shapes=[
            pltpu.VMEM((n_seq, keys + ROPE, latent), BF16),
            pltpu.VMEM((n_blk, rows, latent), BF16),
            pltpu.VMEM((n_blk, rows, ROPE), BF16),
            pltpu.VMEM((heads, latent, VDIM), BF16),
            pltpu.VMEM((n_blk, rows, 1), F32),
            pltpu.VMEM((n_blk, rows, 1), F32),
            pltpu.VMEM((n_blk * rows, latent), F32),
            pltpu.VMEM((latent // 128, n_blk * rows, 128), F32),
            pltpu.VMEM((n_blk * rows, VDIM), F32),
            pltpu.VMEM((n_blk, rows, VDIM), BF16),
            pltpu.VMEM((n_blk, 16, rows), F32),
            pltpu.VMEM((n_blk - 1, rows, VDIM), BF16),
            pltpu.VMEM((n_blk - 1, 16, rows), F32),
            dma((5,)),
            dma((2 * (n_blk - 1),)),
            dma((2 * (n_blk - 1),)),
            dma((nz,)),
            dma((nz,)),
            dma((nz * side,)),
            dma((n_seq,)),
            dma((2 * (n_blk - 1),)),
            dma((2 * (n_blk - 1),)),
        ],
        compiler_params=pltpu.CompilerParams(
            collective_id=0, has_side_effects=True, vmem_limit_bytes=60 * 1024 * 1024
        ),
    )(
        valid_length.reshape(1), accepted, query, rotary, cache_latent, cache_rope,
        draft_latent, draft_rope, ancestors, w_value,
    )
    return (out.reshape(tokens, heads, VDIM), count[0, 0])


def solution(mesh):
    body = functools.partial(shards, mesh.shape["seq"], mesh.shape["blk"])
    return jax.shard_map(
        body,
        mesh=mesh,
        in_specs=(
            P("blk", "seq", None),
            P("blk", None, "seq"),
            P(("seq", "blk"), None),
            P(None, ("seq", "blk")),
            P(),
            P(),
            P(),
            P(),
            P("blk"),
            P("seq", None, None),
        ),
        out_specs=(P("blk", "seq", None), P()),
        check_vma=False,
    )
```

time: 901 us -> 79.4 us (0.09)
  waiting for transfers between devices: 550 us -> 0 us
  blocking collectives: 199 us -> 0 us
  Pallas kernels: 0 us -> 75.2 us
  matrix products: 46.9 us -> 0 us
  starting transfers between devices: 30.3 us -> 0 us
  local copies, waits for them, and re-layouts: 28.4 us -> 2.66 us
  other arithmetic: 22.8 us -> 0 us
  between operations: 14 us -> 1.29 us
    all_to_all x5 -> x0, waiting for transfers between devices: 363 us -> none  [the longest x1 360 us: shards(): lax.all_to_all(latent[None], 'seq', split_axis=1, concat_axis=0, tiled=True)]
    all_gather x3 -> x0, waiting for transfers between devices: 187 us -> none  [the longest x1 125 us: shards(): lax.all_gather(queries, 'seq', axis=1, tiled=True)]
    psum x1 -> x0, blocking collectives: 182 us -> none  [shards(): accepted_total = lax.psum(jnp.sum(accepted), 'blk')]
    pallas_call x0 -> x1, Pallas kernels: none -> 75.2 us  [shards(): pl.pallas_call(functools.partial(kernel, nz, ny, n_blk, tokens, heads), o...]
    dot_general x27 -> x0, matrix products: 46.7 us -> none  [the longest x8 17.3 us: cache_block(): jnp.einsum('hts,sl->htl', weights.astype(jnp.bfloat16), cache_latent, pre...]
    all_to_all x5 -> x0, starting transfers between devices: 30.2 us -> none  [the longest x1 8.66 us: shards(): lax.all_to_all(latent[None], 'seq', split_axis=1, concat_axis=0, tiled=True)]
    all_to_all x5 -> x0, local copies, waits for them, and re-layouts: 18.4 us -> none  [the longest x1 17.7 us: shards(): lax.all_to_all(latent[None], 'seq', split_axis=1, concat_axis=0, tiled=True)]
    reduce_sum x11 -> x0, other arithmetic: 11.9 us -> none  [the longest x1 6.66 us: combine_pieces(): merged = jnp.sum(pieces * factor[:, :, :, None], axis=0)]
  transfers between devices with their start and end apart: 8 -> 0, of which waited for: 6 -> 0; matrix products, arithmetic and copies ran while one was open for 3% -> 0% of each run, Pallas kernels for 0% -> 0%
where the time goes in v1:
time: 79.4 us; the launch traced here: 79.1 us
  Pallas kernels  75.2 us (95%)
  local copies, waits for them, and re-layouts  2.66 us (3%)
  between operations  1.29 us (2%)
    pallas_call x1, Pallas kernels, shards(): pl.pallas_call(functools.partial(kernel, nz, ny, n_blk, tokens, heads), o...  75.2 us

profile of v1, /device:TPU:25, one launch (start us, length us, event | category | flops | bytes accessed | tf_op | source)
XLA Modules:
  0.0 79.1 jit_solution(10818913405909484706)
XLA Ops:
  1.3 75.2 %shard_map.113 = (bf16[256,128]{1,0:T(8,128)(2,1)}, s32[8,1]{1,0:T(8,128)}) custom-call(s32[1]{0:T(128)} %bitcast.7.valid_ref, s32[16]{0:T(128)} %accepted_ref.1, bf16[256,512]{1,0:T(8,128)(2,1)} %bitcast.8, bf16[256,64]{1,0:T(8,128)(2,1)} %bitcast.9, bf16[512,512]{1,0:T(8,128)(2,1)} %kl_ref.1, bf16[64,512]{1,0:T(8,128)(2,1)} %kr_ref.1, ...), custom_call_target="tpu_custom_call" | custom-call | tf_op jit(solution)/shard_map/pallas_call | solution.py:331
  76.5 1.2 %slice.3 = s32[1,1]{1,0:T(1,128)} slice(s32[8,1]{1,0:T(8,128)} %get-tuple-element.5), slice={[0:1], [0:1]} | slice | bytes 8 | tf_op jit(solution)/shard_map/slice | solution.py:370
  77.7 1.5 %copy.14 = bf16[16,16,128]{2,1,0:T(8,128)(2,1)} copy(bf16[16,16,128]{2,1,0:T(8,128)(2,1)} %bitcast.10) | data formatting | bytes 131072

commit v2 on v1

--- a/solution.py
+++ b/solution.py
@@ -43,6 +43,7 @@
     kbuf,
     qbuf,
     qrbuf,
+    rawbuf,
     wbuf,
     top,
     tot,
@@ -74,7 +75,7 @@
         pltpu.make_async_copy(kl_ref, kbuf.at[seq, pl.ds(0, keys)], local_sem.at[0]),
         pltpu.make_async_copy(kr_ref, kbuf.at[seq, pl.ds(keys, ROPE)], local_sem.at[1]),
         pltpu.make_async_copy(q_ref, qbuf.at[blk], local_sem.at[2]),
-        pltpu.make_async_copy(qr_ref, qrbuf.at[blk], local_sem.at[3]),
+        pltpu.make_async_copy(qr_ref, rawbuf, local_sem.at[3]),
         pltpu.make_async_copy(w_ref, wbuf, local_sem.at[4]),
     ]
     for fill in fills:
@@ -85,6 +86,10 @@
 
     def side_peer(j):
         return {"seq": z * ny + lax.rem(y + j, ny)}
+
+    fills[3].wait()
+    turned = [jnp.transpose(rawbuf[t].astype(F32)) for t in range(tokens)]
+    qrbuf[blk] = jnp.concatenate(turned, axis=0).astype(BF16)
 
     barrier = pltpu.get_barrier_semaphore()
     for k in range(1, nb):
@@ -118,38 +123,53 @@
             device_id=where, device_id_type=pl.DeviceIdType.MESH,
         )
 
-    def piece(p, send, where):
-        return remote(kbuf.at[p], kbuf.at[p], send, recv_sem.at[p], where)
-
-    def up(k):
-        return piece(plane(k) * ny + y, up_sem.at[k], {"seq": jnp.minimum(seq + ny, nz * ny - 1)})
-
-    def down(k):
-        return piece(plane(k) * ny + y, down_sem.at[k], {"seq": jnp.maximum(seq - ny, 0)})
-
-    def side(k, j):
-        return piece(plane(k) * ny + y, side_sem.at[k * max(ny - 1, 1) + j - 1], side_peer(j))
-
-    def sends(k, act):
+    cut = (keys + ROPE) // 6 // 16 * 16
+    spans = (pl.ds(0, cut), pl.ds(cut, keys + ROPE - cut))
+
+    def slot(k, j):
+        return plane(k) * ny + lax.rem(y + j, ny)
+
+    def part(p, c, send, where):
+        here = kbuf.at[p, spans[c]]
+        return remote(here, here, send, recv_sem.at[2 * p + c], where)
+
+    def arrived(p, c):
+        part(p, c, recv_sem.at[2 * p + c], {"seq": seq}).wait_recv()
+
+    def along(k, j, c, act):
+        index = 2 * (k * ny + j) + c
+
         @pl.when(jnp.logical_and(plane(k) <= z, z < nz - 1))
         def _():
-            act(up(k))
+            to = {"seq": jnp.minimum(seq + ny, nz * ny - 1)}
+            act(part(slot(k, j), c, up_sem.at[index], to))
 
         @pl.when(jnp.logical_and(plane(k) >= z, z > 0))
         def _():
-            act(down(k))
-
+            to = {"seq": jnp.maximum(seq - ny, 0)}
+            act(part(slot(k, j), c, down_sem.at[index], to))
+
+    def across(k, c, act):
         for j in range(1, ny):
-            act(side(k, j))
+            index = 2 * (k * ny + j) + c
+            act(part(slot(k, 0), c, side_sem.at[index], side_peer(j)))
+
+    def start(copy):
+        copy.start()
+
+    def wait_send(copy):
+        copy.wait_send()
 
     fills[0].wait()
     fills[1].wait()
-    sends(0, lambda c: c.start())
+    for c in range(2):
+        across(0, c, start)
+        along(0, 0, c, start)
 
     def query_copies(k):
         return (
             remote(q_ref, qbuf.at[blk], qsend_sem.at[2 * k - 2], qrecv_sem.at[2 * k - 2], blk_peer(k)),
-            remote(qr_ref, qrbuf.at[blk], qsend_sem.at[2 * k - 1], qrecv_sem.at[2 * k - 1], blk_peer(k)),
+            remote(qrbuf.at[blk], qrbuf.at[blk], qsend_sem.at[2 * k - 1], qrecv_sem.at[2 * k - 1], blk_peer(k)),
         )
 
     for k in range(1, nb):
@@ -165,7 +185,6 @@
 
     lax.fori_loop(0, nb, clear, 0)
     fills[2].wait()
-    fills[3].wait()
     nodes = dl_ref.shape[0]
     dscore = lax.dot_general(qbuf[blk], dl_ref[...], NT, preferred_element_type=F32)
     dscore = dscore + jnp.dot(qrbuf[blk], dr_ref[...], preferred_element_type=F32)
@@ -212,9 +231,14 @@
     def step(k, carry):
         @pl.when(jnp.logical_and(k >= 1, k < nz))
         def _():
-            p = plane(k) * ny + y
-            piece(p, recv_sem.at[p], {"seq": seq}).wait_recv()
-            sends(k, lambda c: c.start())
+            arrived(slot(k, 0), 0)
+            along(k, 0, 0, start)
+            arrived(slot(k, 0), 1)
+            along(k, 0, 1, start)
+            across(k, 1, start)
+            for j in range(1, ny):
+                arrived(slot(k, j), 0)
+                along(k, j, 0, start)
 
         @pl.when(k == 1)
         def _():
@@ -224,13 +248,13 @@
 
         @pl.when(k <= nz)
         def _():
-            attend(plane(k - 1) * ny + y)
+            attend(slot(k - 1, 0))
 
         @pl.when(k >= 2)
         def _():
             def one(j, inner):
-                p = plane(k - 2) * ny + lax.rem(y + j, ny)
-                piece(p, recv_sem.at[p], {"seq": seq}).wait_recv()
+                p = slot(k - 2, j)
+                arrived(p, 1)
                 attend(p)
                 return inner
 
@@ -238,6 +262,9 @@
 
         return carry
 
+    for j in range(1, ny):
+        arrived(slot(0, j), 0)
+        along(0, j, 0, start)
     lax.fori_loop(1, nz + 2, step, 0)
 
     def finish(i, carry):
@@ -299,12 +326,17 @@
     out_ref[...] = (merged / whole).astype(out_ref.dtype)
     for k in range(1, nb):
         count = count + srecv[k - 1, pl.ds(8, 8), :]
-    count_ref[...] = count[:, 0:1].astype(jnp.int32)
+    count_ref[0] = jnp.max(count).astype(jnp.int32)
 
     def drain(k, carry):
-        sends(k, lambda c: c.wait_send())
+        along(k, 0, 0, wait_send)
+        along(k, 0, 1, wait_send)
+        across(k, 1, wait_send)
+        for j in range(1, ny):
+            along(k, j, 0, wait_send)
         return carry
 
+    across(0, 0, wait_send)
     lax.fori_loop(0, nz, drain, 0)
     for k in range(1, nb):
         for c in query_copies(k):
@@ -320,10 +352,8 @@
     keys = cache_latent.shape[0]
     ny = inner_extent(n_seq)
     nz = n_seq // ny
-    side = max(ny - 1, 1)
     assert keys == latent
     query = q_latent.reshape(rows, latent)
-    rotary = jnp.transpose(q_rope, (0, 2, 1)).reshape(rows, ROPE)
     vmem = pl.BlockSpec(memory_space=pltpu.VMEM)
     smem = pl.BlockSpec(memory_space=pltpu.SMEM)
     hbm = pl.BlockSpec(memory_space=pl.ANY)
@@ -332,14 +362,15 @@
         functools.partial(kernel, nz, ny, n_blk, tokens, heads),
         out_shape=(
             jax.ShapeDtypeStruct((rows, VDIM), BF16),
-            jax.ShapeDtypeStruct((8, 1), jnp.int32),
+            jax.ShapeDtypeStruct((1,), jnp.int32),
         ),
         in_specs=[smem, smem, hbm, hbm, hbm, hbm, vmem, vmem, vmem, hbm],
-        out_specs=(vmem, vmem),
+        out_specs=(vmem, smem),
         scratch_shapes=[
             pltpu.VMEM((n_seq, keys + ROPE, latent), BF16),
             pltpu.VMEM((n_blk, rows, latent), BF16),
             pltpu.VMEM((n_blk, rows, ROPE), BF16),
+            pltpu.VMEM((tokens, ROPE, heads), BF16),
             pltpu.VMEM((heads, latent, VDIM), BF16),
             pltpu.VMEM((n_blk, rows, 1), F32),
             pltpu.VMEM((n_blk, rows, 1), F32),
@@ -353,10 +384,10 @@
             dma((5,)),
             dma((2 * (n_blk - 1),)),
             dma((2 * (n_blk - 1),)),
-            dma((nz,)),
-            dma((nz,)),
-            dma((nz * side,)),
-            dma((n_seq,)),
+            dma((2 * n_seq,)),
+            dma((2 * n_seq,)),
+            dma((2 * n_seq,)),
+            dma((2 * n_seq,)),
             dma((2 * (n_blk - 1),)),
             dma((2 * (n_blk - 1),)),
         ],
@@ -364,10 +395,10 @@
             collective_id=0, has_side_effects=True, vmem_limit_bytes=60 * 1024 * 1024
         ),
     )(
-        valid_length.reshape(1), accepted, query, rotary, cache_latent, cache_rope,
+        valid_length.reshape(1), accepted, query, q_rope, cache_latent, cache_rope,
         draft_latent, draft_rope, ancestors, w_value,
     )
-    return (out.reshape(tokens, heads, VDIM), count[0, 0])
+    return (out.reshape(tokens, heads, VDIM), count.reshape(()))
 
 
 def solution(mesh):

time: 79.4 us -> 84.3 us (1.062)
  Pallas kernels: 75.2 us -> 77.9 us
  between operations: 1.29 us -> 2.97 us
    pallas_call x1, Pallas kernels: 75.2 us -> 77.9 us  [shards(): pl.pallas_call(functools.partial(kernel, nz, ny, n_blk, tokens, heads), o...]
    unnamed x1 -> x2, local copies, waits for them, and re-layouts: 1.47 us -> 3.14 us
    slice x1 -> x0, local copies, waits for them, and re-layouts: 1.19 us -> none  [shards(): return (out.reshape(tokens, heads, VDIM), count[0, 0])]
where the time goes in v2:
time: 84.3 us; the launch traced here: 84 us
  Pallas kernels  77.9 us (92%)
  local copies, waits for them, and re-layouts  3.14 us (4%)
  between operations  2.97 us (4%)
    pallas_call x1, Pallas kernels, shards(): pl.pallas_call(functools.partial(kernel, nz, ny, n_blk, tokens, heads), o...  77.9 us
    unnamed x2, local copies, waits for them, and re-layouts  3.14 us

profile of v2, /device:TPU:25, one launch (start us, length us, event | category | flops | bytes accessed | tf_op | source)
XLA Modules:
  0.0 84.0 jit_solution(4920048318706700291)
XLA Ops:
  1.3 1.7 %copy.12.qr_ref = bf16[16,64,16]{2,1,0:T(8,128)(2,1)} copy(bf16[16,64,16]{1,2,0:T(8,128)(2,1)} %param.11) | data formatting | bytes 65536 | tf_op args[1]
  2.9 77.9 %shard_map.113 = (bf16[256,128]{1,0:T(8,128)(2,1)}, s32[1]{0:T(128)}) custom-call(s32[1]{0:T(128)} %bitcast.4.valid_ref, s32[16]{0:T(128)} %accepted_ref.1, bf16[256,512]{1,0:T(8,128)(2,1)} %bitcast.5, bf16[16,64,16]{2,1,0:T(8,128)(2,1)} %copy.12.qr_ref, bf16[512,512]{1,0:T(8,128)(2,1)} %kl_ref.1, bf16[64,512]{1,0:T(8,128)(2,1)} %kr_ref.1, ...), custom_call_target="tpu_custom_call" | custom-call | tf_op jit(solution)/shard_map/pallas_call | solution.py:361
  80.8 1.5 %copy.16 = bf16[16,16,128]{2,1,0:T(8,128)(2,1)} copy(bf16[16,16,128]{2,1,0:T(8,128)(2,1)} %bitcast.6) | data formatting | bytes 131072

commit v3 on v2

--- a/solution.py
+++ b/solution.py
@@ -9,6 +9,7 @@
 
 ROPE = 64
 VDIM = 128
+PARTS = 6
 NEG = -1e30
 F32 = jnp.float32
 BF16 = jnp.bfloat16
@@ -123,21 +124,20 @@
             device_id=where, device_id_type=pl.DeviceIdType.MESH,
         )
 
-    cut = (keys + ROPE) // 6 // 16 * 16
-    spans = (pl.ds(0, cut), pl.ds(cut, keys + ROPE - cut))
+    size = (keys + ROPE) // PARTS
 
     def slot(k, j):
         return plane(k) * ny + lax.rem(y + j, ny)
 
     def part(p, c, send, where):
-        here = kbuf.at[p, spans[c]]
-        return remote(here, here, send, recv_sem.at[2 * p + c], where)
+        here = kbuf.at[p, pl.ds(pl.multiple_of(c * size, 16), size)]
+        return remote(here, here, send, recv_sem.at[PARTS * p + c], where)
 
     def arrived(p, c):
-        part(p, c, recv_sem.at[2 * p + c], {"seq": seq}).wait_recv()
+        part(p, c, recv_sem.at[PARTS * p + c], {"seq": seq}).wait_recv()
 
     def along(k, j, c, act):
-        index = 2 * (k * ny + j) + c
+        index = PARTS * (k * ny + j) + c
 
         @pl.when(jnp.logical_and(plane(k) <= z, z < nz - 1))
         def _():
@@ -151,7 +151,7 @@
 
     def across(k, c, act):
         for j in range(1, ny):
-            index = 2 * (k * ny + j) + c
+            index = PARTS * (k * ny + j) + c
             act(part(slot(k, 0), c, side_sem.at[index], side_peer(j)))
 
     def start(copy):
@@ -162,7 +162,7 @@
 
     fills[0].wait()
     fills[1].wait()
-    for c in range(2):
+    for c in range(PARTS):
         across(0, c, start)
         along(0, 0, c, start)
 
@@ -203,9 +203,9 @@
     )
     valid = valid_ref[0]
 
-    def attend(p):
-        start = (p * nb + blk) * keys
-        live = start + lax.broadcasted_iota(jnp.int32, (1, keys), 1) < valid
+    def attend(p, low, high):
+        first_key = (p * nb + blk) * keys
+        live = first_key + lax.broadcasted_iota(jnp.int32, (1, keys), 1) < valid
 
         def block(i, carry):
             key = kbuf[p, pl.ds(0, keys), :]
@@ -226,39 +226,55 @@
             )
             return carry
 
-        lax.fori_loop(0, nb, block, 0)
+        lax.fori_loop(low, high, block, 0)
 
     def step(k, carry):
-        @pl.when(jnp.logical_and(k >= 1, k < nz))
+        def turn(c, inner):
+            @pl.when(k < nz)
+            def _():
+                arrived(slot(k, 0), c)
+                along(k, 0, c, start)
+
+                @pl.when(c > 0)
+                def _():
+                    across(k, c, start)
+
+            low, high = c * nb // PARTS, (c + 1) * nb // PARTS
+
+            @pl.when(jnp.logical_and(k >= 2, c == 0))
+            def _():
+                for j in range(1, ny):
+                    for other in range(1, PARTS):
+                        arrived(slot(k - 2, j), other)
+
+            def own_line(n, x):
+                attend(slot(jnp.where(n == 0, 0, k - 1), 0), low, high)
+                return x
+
+            lax.fori_loop(
+                jnp.where(k == 2, 0, 1), jnp.where(jnp.logical_and(k >= 2, k <= nz), 2, 1), own_line, 0
+            )
+
+            def other_line(j, x):
+                attend(slot(k - 2, j), low, high)
+                return x
+
+            lax.fori_loop(1, jnp.where(k >= 2, ny, 1), other_line, 0)
+            return inner
+
+        @pl.when(k == 2)
         def _():
-            arrived(slot(k, 0), 0)
-            along(k, 0, 0, start)
-            arrived(slot(k, 0), 1)
-            along(k, 0, 1, start)
-            across(k, 1, start)
+            for j in range(1, nb):
+                for copy in query_copies(j):
+                    copy.wait_recv()
+
+        lax.fori_loop(0, PARTS, turn, 0)
+
+        @pl.when(k < nz)
+        def _():
             for j in range(1, ny):
                 arrived(slot(k, j), 0)
                 along(k, j, 0, start)
-
-        @pl.when(k == 1)
-        def _():
-            for j in range(1, nb):
-                for c in query_copies(j):
-                    c.wait_recv()
-
-        @pl.when(k <= nz)
-        def _():
-            attend(slot(k - 1, 0))
-
-        @pl.when(k >= 2)
-        def _():
-            def one(j, inner):
-                p = slot(k - 2, j)
-                arrived(p, 1)
-                attend(p)
-                return inner
-
-            lax.fori_loop(1, ny, one, 0)
 
         return carry
 
@@ -329,9 +345,10 @@
     count_ref[0] = jnp.max(count).astype(jnp.int32)
 
     def drain(k, carry):
-        along(k, 0, 0, wait_send)
-        along(k, 0, 1, wait_send)
-        across(k, 1, wait_send)
+        for c in range(PARTS):
+            along(k, 0, c, wait_send)
+            if c > 0:
+                across(k, c, wait_send)
         for j in range(1, ny):
             along(k, j, 0, wait_send)
         return carry
@@ -352,7 +369,7 @@
     keys = cache_latent.shape[0]
     ny = inner_extent(n_seq)
     nz = n_seq // ny
-    assert keys == latent
+    assert keys == latent and (keys + ROPE) % (16 * PARTS) == 0
     query = q_latent.reshape(rows, latent)
     vmem = pl.BlockSpec(memory_space=pltpu.VMEM)
     smem = pl.BlockSpec(memory_space=pltpu.SMEM)
@@ -384,10 +401,10 @@
             dma((5,)),
             dma((2 * (n_blk - 1),)),
             dma((2 * (n_blk - 1),)),
-            dma((2 * n_seq,)),
-            dma((2 * n_seq,)),
-            dma((2 * n_seq,)),
-            dma((2 * n_seq,)),
+            dma((PARTS * n_seq,)),
+            dma((PARTS * n_seq,)),
+            dma((PARTS * n_seq,)),
+            dma((PARTS * n_seq,)),
             dma((2 * (n_blk - 1),)),
             dma((2 * (n_blk - 1),)),
         ],

time: 84.3 us -> 78.2 us (0.928)
  Pallas kernels: 77.9 us -> 71.3 us
    pallas_call x1, Pallas kernels: 77.9 us -> 71.3 us  [shards(): pl.pallas_call(functools.partial(kernel, nz, ny, n_blk, tokens, heads), o...]
where the time goes in v3:
time: 78.2 us; the launch traced here: 77.5 us
  Pallas kernels  71.3 us (91%)
  local copies, waits for them, and re-layouts  3.14 us (4%)
  between operations  2.97 us (4%)
    pallas_call x1, Pallas kernels, shards(): pl.pallas_call(functools.partial(kernel, nz, ny, n_blk, tokens, heads), o...  71.3 us
    unnamed x2, local copies, waits for them, and re-layouts  3.14 us

profile of v3, /device:TPU:25, one launch (start us, length us, event | category | flops | bytes accessed | tf_op | source)
XLA Modules:
  0.0 77.5 jit_solution(15741759327460084684)
XLA Ops:
  1.3 1.7 %copy.12.qr_ref = bf16[16,64,16]{2,1,0:T(8,128)(2,1)} copy(bf16[16,64,16]{1,2,0:T(8,128)(2,1)} %param.11) | data formatting | bytes 65536 | tf_op args[1]
  2.9 71.3 %shard_map.113 = (bf16[256,128]{1,0:T(8,128)(2,1)}, s32[1]{0:T(128)}) custom-call(s32[1]{0:T(128)} %bitcast.4.valid_ref, s32[16]{0:T(128)} %accepted_ref.1, bf16[256,512]{1,0:T(8,128)(2,1)} %bitcast.5, bf16[16,64,16]{2,1,0:T(8,128)(2,1)} %copy.12.qr_ref, bf16[512,512]{1,0:T(8,128)(2,1)} %kl_ref.1, bf16[64,512]{1,0:T(8,128)(2,1)} %kr_ref.1, ...), custom_call_target="tpu_custom_call" | custom-call | tf_op jit(solution)/shard_map/pallas_call | solution.py:378
  74.3 1.5 %copy.16 = bf16[16,16,128]{2,1,0:T(8,128)(2,1)} copy(bf16[16,16,128]{2,1,0:T(8,128)(2,1)} %bitcast.6) | data formatting | bytes 131072

commit v4 on v3

--- a/solution.py
+++ b/solution.py
@@ -44,7 +44,6 @@
     kbuf,
     qbuf,
     qrbuf,
-    rawbuf,
     wbuf,
     top,
     tot,
@@ -76,7 +75,7 @@
         pltpu.make_async_copy(kl_ref, kbuf.at[seq, pl.ds(0, keys)], local_sem.at[0]),
         pltpu.make_async_copy(kr_ref, kbuf.at[seq, pl.ds(keys, ROPE)], local_sem.at[1]),
         pltpu.make_async_copy(q_ref, qbuf.at[blk], local_sem.at[2]),
-        pltpu.make_async_copy(qr_ref, rawbuf, local_sem.at[3]),
+        pltpu.make_async_copy(qr_ref, qrbuf.at[blk], local_sem.at[3]),
         pltpu.make_async_copy(w_ref, wbuf, local_sem.at[4]),
     ]
     for fill in fills:
@@ -87,10 +86,6 @@
 
     def side_peer(j):
         return {"seq": z * ny + lax.rem(y + j, ny)}
-
-    fills[3].wait()
-    turned = [jnp.transpose(rawbuf[t].astype(F32)) for t in range(tokens)]
-    qrbuf[blk] = jnp.concatenate(turned, axis=0).astype(BF16)
 
     barrier = pltpu.get_barrier_semaphore()
     for k in range(1, nb):
@@ -169,7 +164,7 @@
     def query_copies(k):
         return (
             remote(q_ref, qbuf.at[blk], qsend_sem.at[2 * k - 2], qrecv_sem.at[2 * k - 2], blk_peer(k)),
-            remote(qrbuf.at[blk], qrbuf.at[blk], qsend_sem.at[2 * k - 1], qrecv_sem.at[2 * k - 1], blk_peer(k)),
+            remote(qr_ref, qrbuf.at[blk], qsend_sem.at[2 * k - 1], qrecv_sem.at[2 * k - 1], blk_peer(k)),
         )
 
     for k in range(1, nb):
@@ -185,6 +180,7 @@
 
     lax.fori_loop(0, nb, clear, 0)
     fills[2].wait()
+    fills[3].wait()
     nodes = dl_ref.shape[0]
     dscore = lax.dot_general(qbuf[blk], dl_ref[...], NT, preferred_element_type=F32)
     dscore = dscore + jnp.dot(qrbuf[blk], dr_ref[...], preferred_element_type=F32)
@@ -371,6 +367,7 @@
     nz = n_seq // ny
     assert keys == latent and (keys + ROPE) % (16 * PARTS) == 0
     query = q_latent.reshape(rows, latent)
+    rotary = jnp.transpose(q_rope, (0, 2, 1)).reshape(rows, ROPE)
     vmem = pl.BlockSpec(memory_space=pltpu.VMEM)
     smem = pl.BlockSpec(memory_space=pltpu.SMEM)
     hbm = pl.BlockSpec(memory_space=pl.ANY)
@@ -387,7 +384,6 @@
             pltpu.VMEM((n_seq, keys + ROPE, latent), BF16),
             pltpu.VMEM((n_blk, rows, latent), BF16),
             pltpu.VMEM((n_blk, rows, ROPE), BF16),
-            pltpu.VMEM((tokens, ROPE, heads), BF16),
             pltpu.VMEM((heads, latent, VDIM), BF16),
             pltpu.VMEM((n_blk, rows, 1), F32),
             pltpu.VMEM((n_blk, rows, 1), F32),
@@ -412,7 +408,7 @@
             collective_id=0, has_side_effects=True, vmem_limit_bytes=60 * 1024 * 1024
         ),
     )(
-        valid_length.reshape(1), accepted, query, q_rope, cache_latent, cache_rope,
+        valid_length.reshape(1), accepted, query, rotary, cache_latent, cache_rope,
         draft_latent, draft_rope, ancestors, w_value,
     )
     return (out.reshape(tokens, heads, VDIM), count.reshape(()))

time: 78.2 us -> 75.3 us (0.963)
  local copies, waits for them, and re-layouts: 3.14 us -> 1.47 us
  Pallas kernels: 71.3 us -> 70 us
    unnamed x2 -> x1, local copies, waits for them, and re-layouts: 3.14 us -> 1.47 us
    pallas_call x1, Pallas kernels: 71.3 us -> 70 us  [shards(): pl.pallas_call(functools.partial(kernel, nz, ny, n_blk, tokens, heads), o...]
where the time goes in v4:
time: 75.3 us; the launch traced here: 74.5 us
  Pallas kernels  70 us (93%)
  between operations  3.03 us (4%)
  local copies, waits for them, and re-layouts  1.47 us (2%)
    pallas_call x1, Pallas kernels, shards(): pl.pallas_call(functools.partial(kernel, nz, ny, n_blk, tokens, heads), o...  70 us

profile of v4, /device:TPU:25, one launch (start us, length us, event | category | flops | bytes accessed | tf_op | source)
XLA Modules:
  0.0 74.5 jit_solution(11107119707041614243)
XLA Ops:
  1.3 70.0 %shard_map.113 = (bf16[256,128]{1,0:T(8,128)(2,1)}, s32[1]{0:T(128)}) custom-call(s32[1]{0:T(128)} %bitcast.7.valid_ref, s32[16]{0:T(128)} %accepted_ref.1, bf16[256,512]{1,0:T(8,128)(2,1)} %bitcast.8, bf16[256,64]{1,0:T(8,128)(2,1)} %bitcast.9, bf16[512,512]{1,0:T(8,128)(2,1)} %kl_ref.1, bf16[64,512]{1,0:T(8,128)(2,1)} %kr_ref.1, bf16[64,512]{1,0:T(8,128)(2,1)} %dl_ref.1, ...), custom_call_target="tpu_custom_call" | custom-call | tf_op jit(solution)/shard_map/pallas_call | solution.py:375
  71.3 1.5 %copy.15 = bf16[16,16,128]{2,1,0:T(8,128)(2,1)} copy(bf16[16,16,128]{2,1,0:T(8,128)(2,1)} %bitcast.10) | data formatting | bytes 131072
